TPU v7x, 32 devices: a whole 2x2x4 slice. The times are simulated.
32 devices in a mesh: member: 2 (over x), ty: 16 (over z, y, core).
Axes of the slice: x: 2, y: 2, z: 4, core: 2. Of those that a mesh axis runs over, the one named last changes fastest.
Arguments:
- fields: float32 [32, 768, 6, 768], P('member', 'ty'), parts along dimension 0, may hold values from -6 to 6
- damp_four: float32 [32], P('member'), parts along dimension 0, may hold values from 0.004 to 0.03
- damp_six: float32 [32], P('member'), parts along dimension 0, may hold values from 0.0008 to 0.006
- metric: float32 [4, 768, 6, 768], P(None, 'ty'), may hold values from 0.1 to 1.9
- seam_table: int32 [6, 4, 3], replicated, may hold values from 0 to 5
Outputs:
- damped: float32 [32, 768, 6, 768], P('member', 'ty'), parts along dimension 0
There are 2 independent parts, one for each index of `member`. A program takes and returns all parts, laid end to end along the dimension named above; an argument that names none is the same for every part. Nothing has to cross between parts.
Inputs may be any that keep to these rules, and one draw needn't show every extreme that they name: The table describes the surface of a cube with every face seen from outside: the joining is symmetric, no face is joined to itself, and r is 1 exactly when both edges are among (south, east) or both among (north, west).
All inputs are finite; a program needn't handle non-finite values.
Results may differ from a plain program's by a relative error of at most 0.00005.
Values sent between devices are 32-bit elements; how exact they have to be, the bound alone decides.
A program may use at most 128 MiB of HBM per device.

v0:
```python
import jax
import jax.numpy as jnp
from jax import lax
from jax.sharding import PartitionSpec as P


def with_halo(cells, sides, width):
    for axis, dim in sides:
        count = lax.axis_size(axis)
        ends = count - 1
        head = lax.slice_in_dim(cells, 0, width, axis=dim)
        tail = lax.slice_in_dim(cells, cells.shape[dim] - width, cells.shape[dim], axis=dim)
        cells = jnp.concatenate(
            [
                lax.ppermute(tail, axis, [(i, (i + 1) % count) for i in range(ends)]),
                cells,
                lax.ppermute(head, axis, [((i + 1) % count, i) for i in range(ends)]),
            ],
            axis=dim,
        )
    return cells


def strip_edges(source):
    east_cells = jnp.transpose(source[:, :, :, -1], (0, 2, 1))
    west_cells = jnp.transpose(source[:, :, :, 0], (0, 2, 1))
    return jnp.stack([east_cells, west_cells], axis=2)


def gather_edges(source):
    tile_index = lax.axis_index("ty")
    tile_count = lax.axis_size("ty")
    strip_rows = source.shape[1]
    row_width = source.shape[3]
    strip_cells = strip_edges(source)
    first_row = jnp.where(tile_index == 0, source[:, 0], 0.0)
    last_row = jnp.where(tile_index == tile_count - 1, source[:, -1], 0.0)
    blank = jnp.zeros(strip_cells.shape[:3] + (row_width,), jnp.float32)
    placed = lax.dynamic_update_slice_in_dim(blank, strip_cells, tile_index * strip_rows, 3)
    rim_cells = jnp.stack([first_row, placed[:, :, 0], last_row, placed[:, :, 1]], axis=2)
    edge_set = lax.psum(rim_cells, "ty")
    return edge_set


def seam_halo(edge_set, seam_table):
    levels = edge_set.shape[0]
    row_width = edge_set.shape[3]
    flattened = edge_set.reshape(levels, 24, row_width)
    picked = (seam_table[:, :, 0] * 4 + seam_table[:, :, 1]).reshape(24)
    onehot = (picked[:, None] == jnp.arange(24, dtype=jnp.int32)[None, :]).astype(jnp.float32)
    neighbor = jnp.einsum("jk,lkc->ljc", onehot, flattened, precision=lax.Precision.HIGHEST)
    neighbor = neighbor.reshape(levels, 6, 4, row_width)
    flipped = (seam_table[:, :, 2] == 1)[None, :, :, None]
    return jnp.where(flipped, neighbor[..., ::-1], neighbor)


def laplace(source, metric, seam_table):
    tile_index = lax.axis_index("ty")
    tile_count = lax.axis_size("ty")
    strip_rows = source.shape[1]
    padded = with_halo(source, (("ty", 1),), 1)
    halo_cells = seam_halo(gather_edges(source), seam_table)
    south_row = jnp.where(tile_index == 0, halo_cells[:, :, 0], padded[:, 0])
    north_row = jnp.where(tile_index == tile_count - 1, halo_cells[:, :, 2], padded[:, -1])
    row_start = tile_index * strip_rows
    west_cells = jnp.transpose(
        lax.dynamic_slice_in_dim(halo_cells[:, :, 3], row_start, strip_rows, 2), (0, 2, 1)
    )[..., None]
    east_cells = jnp.transpose(
        lax.dynamic_slice_in_dim(halo_cells[:, :, 1], row_start, strip_rows, 2), (0, 2, 1)
    )[..., None]
    padded_x = jnp.concatenate([west_cells, source, east_cells], axis=3)
    padded_y = jnp.concatenate([south_row[:, None], source, north_row[:, None]], axis=1)
    return (
        metric[0] * (padded_x[..., :-2] - source)
        + metric[1] * (padded_x[..., 2:] - source)
        + metric[2] * (padded_y[:, :-2] - source)
        + metric[3] * (padded_y[:, 2:] - source)
    )


def per_device(fields, damp_four, damp_six, metric, seam_table):
    second = laplace(fields, metric, seam_table)
    fourth = laplace(second, metric, seam_table)
    sixth = laplace(fourth, metric, seam_table)
    return fields - damp_four[:, None, None, None] * fourth + damp_six[:, None, None, None] * sixth


def solution(mesh):
    placed = (
        P("member", "ty", None, None),
        P("member"),
        P("member"),
        P(None, "ty", None, None),
        P(),
    )
    return jax.shard_map(
        per_device,
        mesh=mesh,
        in_specs=placed,
        out_specs=P("member", "ty", None, None),
        check_vma=False,
    )
```

profile of v0, /device:TPU:0, one launch (start us, length us, event | category | flops | bytes accessed | tf_op | source)
XLA Modules:
  0.0 596.8 jit_solution(6882728278029485408)
XLA Ops:
  6.5 4.6 fusion.54
  11.1 18.5 %copy.89 = f32[16,48,6,768]{3,0,2,1:T(8,128)} copy(f32[16,48,6,768]{3,1,2,0:T(8,128)} %param.5) | data formatting | bytes 28311552 | tf_op args[0]
  38.1 4.7 collective-permute-start
  49.8 88.0 %all-reduce.4.cloned.1.call-done = f32[16,24,768]{2,1,0:T(8,128)} async-done(((f32[16,24,768]{2,1,0:T(8,128)}), f32[16,24,768]{2,1,0:T(8,128)}) %all-reduce.4.cloned.1.call-update) | async-done | bytes 1179664 | tf_op jit(solution)/shard_map/psum | solution.py:41
  141.1 4.7 rev.9
  150.1 3.9 copy.68
  155.7 4.0 copy.73
  161.7 33.4 %fusion.26 = f32[16,48,6,768]{3,0,2,1:T(8,128)} fusion(f32[16,48,6,768]{3,0,2,1:T(8,128)} %copy.89, f32[16,1,6,768]{3,0,2,1:T(8,128)} %get-tuple-element.38, f32[16,1,6,768]{3,0,2,1:T(8,128)} %get-tuple-element.37, f32[16,48,6,1]{3,0,2,1:T(8,128)} %copy.73, f32[16,48,6,1]{3,0,2,1:T(8,128)} %copy.68, f32[48,6,768]{2,1,0:T(8,128)} %copy.79, ...), kind=kLoop, calls=%fused_computation.35 | loop fusion | flops 53084160 | bytes 32477184 | tf_op jit(solution)/shard_map/add | solution.py:75
  195.1 5.3 fusion.52
  205.9 3.4 copy.83
  224.6 91.8 %all-reduce.6.cloned.1.call-done = f32[16,24,768]{2,1,0:T(8,128)} async-done(((f32[16,24,768]{2,1,0:T(8,128)}), f32[16,24,768]{2,1,0:T(8,128)}) %all-reduce.6.cloned.1.call-update) | async-done | bytes 1179664 | tf_op jit(solution)/shard_map/psum | solution.py:41
  319.3 10.9 %reshape.133 = f32[16,6,4,768]{3,2,1,0:T(4,128)} reshape(f32[16,24,768]{2,1,0:T(8,128)} %convolution_bitcast_fusion.1) | data formatting | bytes 2359296 | tf_op jit(solution)/shard_map/reshape | solution.py:52
  332.9 4.7 rev.10
  342.1 3.9 copy.87
  347.7 4.0 copy.88
  353.7 34.7 %fusion.15 = f32[16,48,6,768]{3,0,2,1:T(8,128)} fusion(f32[16,48,6,768]{3,0,2,1:T(8,128)} %fusion.26, f32[16,1,6,768]{3,0,2,1:T(8,128)} %get-tuple-element.34, f32[16,1,6,768]{3,0,2,1:T(8,128)} %get-tuple-element.33, f32[16,48,6,1]{3,0,2,1:T(8,128)} %copy.88, f32[16,48,6,1]{3,0,2,1:T(8,128)} %copy.87, f32[48,6,768]{2,1,0:T(8,128)} %copy.79, ...), kind=kLoop, calls=%fused_computation.20 | loop fusion | flops 53084160 | bytes 32477184 | tf_op jit(solution)/shard_map/add | solution.py:75
  388.4 5.3 fusion.50
  395.8 3.4 copy.90
  418.1 91.7 %all-reduce.8.cloned.1.call-done = f32[16,24,768]{2,1,0:T(8,128)} async-done(((f32[16,24,768]{2,1,0:T(8,128)}), f32[16,24,768]{2,1,0:T(8,128)}) %all-reduce.8.cloned.1.call-update) | async-done | bytes 1179664 | tf_op jit(solution)/shard_map/psum | solution.py:41
  518.0 4.7 rev.11
  526.5 3.9 copy.97
  530.5 4.0 copy.98
  536.0 35.3 %fusion.4 = f32[16,48,6,768]{3,0,2,1:T(8,128)} fusion(f32[16,48,6,768]{3,0,2,1:T(8,128)} %fusion.15, f32[16,1,6,768]{3,0,2,1:T(8,128)S(1)} %get-tuple-element.30, f32[16,1,6,768]{3,0,2,1:T(8,128)S(1)} %get-tuple-element.29, f32[16,48,6,1]{3,0,2,1:T(8,128)} %copy.98, f32[16,48,6,1]{3,0,2,1:T(8,128)} %copy.97, f32[16]{0:T(128)S(1)} %copy-done.5, ...), kind=kLoop, calls=%fused_computation.5 | loop fusion | flops 67239936 | bytes 46633088 | tf_op jit(solution)/shard_map/add | solution.py:86
  571.3 18.5 %copy.99 = f32[16,48,6,768]{3,1,2,0:T(8,128)} copy(f32[16,48,6,768]{3,0,2,1:T(8,128)} %fusion.4) | data formatting | bytes 28311552 | tf_op jit(solution)/shard_map/add | solution.py:86
  (91 shorter events, 95.5 us)
Async XLA Ops:
  6.5 131.3 %all-reduce.4.cloned.1.call-start = ((), (), s32[]{:S(2)}) async-start(), calls=%async_computation | async-start | bytes 2359296 | tf_op jit(solution)/shard_map/psum | solution.py:41
  36.6 7.5 %copy-start.4 = (s32[6,4,3]{0,1,2:T(4,128)S(1)}, s32[6,4,3]{0,1,2:T(4,128)}, u32[]{:S(2)}) copy-start(s32[6,4,3]{0,1,2:T(4,128)} %param.9) | copy-start | bytes 868
  38.0 278.3 %all-reduce.6.cloned.1.call-start = ((), (), s32[]{:S(2)}) async-start(), calls=%async_computation.1 | async-start | bytes 2359296 | tf_op jit(solution)/shard_map/psum | solution.py:41
  38.1 121.6 %collective-permute-start = (f32[16,1,6,768]{3,0,2,1:T(8,128)}, f32[16,1,6,768]{3,0,2,1:T(8,128)}, u32[]{:S(2)}, u32[]{:S(2)}) collective-permute-start(f32[16,1,6,768]{3,0,2,1:T(8,128)} %get-tuple-element.17), channel_id=1, source_target_pairs={{0,1},{1,2},{2,3},{3,4},{4,5},{5,6},{6,7},{7,8},{8,9},{9,10},{10,1... | collective-permute-start | bytes 884744 | tf_op jit(solution)/shard_map/ppermute | solution.py:15
  42.8 116.8 %collective-permute-start.1 = (f32[16,1,6,768]{3,0,2,1:T(8,128)}, f32[16,1,6,768]{3,0,2,1:T(8,128)}, u32[]{:S(2)}, u32[]{:S(2)}) collective-permute-start(f32[16,1,6,768]{3,0,2,1:T(8,128)} %get-tuple-element.19), channel_id=1, source_target_pairs={{1,0},{2,1},{3,2},{4,3},{5,4},{6,5},{7,6},{8,7},{9,8},{10,9},{11,1... | collective-permute-start | bytes 884744 | tf_op jit(solution)/shard_map/ppermute | solution.py:17
  147.7 1.0 copy-start.2
  220.0 289.8 %all-reduce.8.cloned.1.call-start = ((), (), s32[]{:S(2)}) async-start(), calls=%async_computation.2 | async-start | bytes 2359296 | tf_op jit(solution)/shard_map/psum | solution.py:41
  220.1 131.6 %collective-permute-start.2 = (f32[16,1,6,768]{3,0,2,1:T(8,128)}, f32[16,1,6,768]{3,0,2,1:T(8,128)}, u32[]{:S(2)}, u32[]{:S(2)}) collective-permute-start(f32[16,1,6,768]{3,0,2,1:T(8,128)} %get-tuple-element.11), channel_id=1, source_target_pairs={{0,1},{1,2},{2,3},{3,4},{4,5},{5,6},{6,7},{7,8},{8,9},{9,10},{10,1... | collective-permute-start | bytes 884744 | tf_op jit(solution)/shard_map/ppermute | solution.py:15
  223.3 128.3 %collective-permute-start.3 = (f32[16,1,6,768]{3,0,2,1:T(8,128)}, f32[16,1,6,768]{3,0,2,1:T(8,128)}, u32[]{:S(2)}, u32[]{:S(2)}) collective-permute-start(f32[16,1,6,768]{3,0,2,1:T(8,128)} %get-tuple-element.14), channel_id=1, source_target_pairs={{1,0},{2,1},{3,2},{4,3},{5,4},{6,5},{7,6},{8,7},{9,8},{10,9},{11,1... | collective-permute-start | bytes 884744 | tf_op jit(solution)/shard_map/ppermute | solution.py:17
  339.7 1.0 copy-start.3
  413.6 120.9 %collective-permute-start.4 = (f32[16,1,6,768]{3,0,2,1:T(8,128)}, f32[16,1,6,768]{3,0,2,1:T(8,128)}, u32[]{:S(2)}, u32[]{:S(2)}) collective-permute-start(f32[16,1,6,768]{3,0,2,1:T(8,128)} %get-tuple-element.5), channel_id=1, source_target_pairs={{0,1},{1,2},{2,3},{3,4},{4,5},{5,6},{6,7},{7,8},{8,9},{9,10},{10,1... | collective-permute-start | bytes 884744 | tf_op jit(solution)/shard_map/ppermute | solution.py:15
  416.8 117.7 %collective-permute-start.5 = (f32[16,1,6,768]{3,0,2,1:T(8,128)}, f32[16,1,6,768]{3,0,2,1:T(8,128)}, u32[]{:S(2)}, u32[]{:S(2)}) collective-permute-start(f32[16,1,6,768]{3,0,2,1:T(8,128)} %get-tuple-element.8), channel_id=1, source_target_pairs={{1,0},{2,1},{3,2},{4,3},{5,4},{6,5},{7,6},{8,7},{9,8},{10,9},{11,1... | collective-permute-start | bytes 884744 | tf_op jit(solution)/shard_map/ppermute | solution.py:17
  524.7 1.0 copy-start.1
  530.5 5.4 copy-start.5
  530.5 5.4 copy-start.6
  534.5 1.5 copy-start
Sparse Core Ops, SparseCore 0:
  38.2 99.5 all-reduce.3
  220.1 96.1 all-reduce.5
  413.7 96.0 all-reduce.7
where the time goes:
time: 606 us; the launch traced here: 597 us
  waiting for transfers between devices  271 us (45%)
  local copies, waits for them, and re-layouts  162 us (27%)
  other arithmetic  126 us (21%)
  starting transfers between devices  15.1 us (2%)
  between operations  13.8 us (2%)
  matrix products  7.85 us (1%)
    psum x3, waiting for transfers between devices, gather_edges(): edge_set = lax.psum(rim_cells, 'ty')  271 us
    add x2, other arithmetic, laplace(): metric[0] * (padded_x[..., :-2] - source)  68.1 us
    add x1, other arithmetic, per_device(): fields - damp_four[:, None, None, None] * fourth  35.3 us
    unnamed x19, local copies, waits for them, and re-layouts  28.6 us
    reshape x5, local copies, waits for them, and re-layouts, seam_halo(): neighbor = neighbor.reshape(levels, 6, 4, row_width)  20.2 us
    slice x4, local copies, waits for them, and re-layouts, strip_edges(): east_cells = jnp.transpose(source[:, :, :, -1], (0, 2, 1))  18.6 us
    add x1, local copies, waits for them, and re-layouts, per_device(): fields - damp_four[:, None, None, None] * fourth  18.5 us
    broadcast_in_dim x6, local copies, waits for them, and re-layouts, laplace(): jnp.transpose(lax.dynamic_slice_in_dim(halo_cells[:, :, 1], row_start, st...  15.9 us
  transfers between devices with their start and end apart: 9, of which 3 were waited for; matrix products, arithmetic and copies ran while one was open for 14% of the time, Pallas kernels for 0%

commit v1 on v0

--- a/solution.py
+++ b/solution.py
@@ -38,7 +38,9 @@
     blank = jnp.zeros(strip_cells.shape[:3] + (row_width,), jnp.float32)
     placed = lax.dynamic_update_slice_in_dim(blank, strip_cells, tile_index * strip_rows, 3)
     rim_cells = jnp.stack([first_row, placed[:, :, 0], last_row, placed[:, :, 1]], axis=2)
-    edge_set = lax.psum(rim_cells, "ty")
+    edge_set = rim_cells
+    for hop in (1, 2, 4, 8):
+        edge_set = edge_set + lax.ppermute(edge_set, "ty", [(dev, dev ^ hop) for dev in range(16)])
     return edge_set
 
 

time: 606 us -> 628 us (1.036)
  starting transfers between devices: 15.1 us -> 43.5 us
  waiting for transfers between devices: 271 us -> 292 us
  local copies, waits for them, and re-layouts: 162 us -> 145 us
  between operations: 13.8 us -> 0.75 us
    ppermute x0 -> x12, waiting for transfers between devices: none -> 292 us  [gather_edges(): lax.ppermute(edge_set, 'ty', [(dev, dev ^ hop) for dev in range(16)])]
    psum x3 -> x0, waiting for transfers between devices: 271 us -> none  [gather_edges(): edge_set = lax.psum(rim_cells, 'ty')]
    ppermute x0 -> x12, starting transfers between devices: none -> 23.4 us  [gather_edges(): lax.ppermute(edge_set, 'ty', [(dev, dev ^ hop) for dev in range(16)])]
    ppermute x3, starting transfers between devices: 3.84 us -> 14.1 us  [with_halo(): lax.ppermute(head, axis, [((i + 1) % count, i) for i in range(ends)])]
    reshape x3 -> x0, local copies, waits for them, and re-layouts: 6.85 us -> none  [seam_halo(): flattened = edge_set.reshape(levels, 24, row_width)]
    reshape x5 -> x6, local copies, waits for them, and re-layouts: 20.2 us -> 15.8 us  [seam_halo(): neighbor = neighbor.reshape(levels, 6, 4, row_width)]
    unnamed x19 -> x28, local copies, waits for them, and re-layouts: 28.6 us -> 28.6 us
  transfers between devices with their start and end apart: 9 -> 18, of which waited for: 3 -> 12; matrix products, arithmetic and copies ran while one was open for 14% -> 13% of each run, Pallas kernels for 0% -> 0%
where the time goes in v1:
time: 628 us; the launch traced here: 618 us
  waiting for transfers between devices  292 us (46%)
  local copies, waits for them, and re-layouts  145 us (23%)
  other arithmetic  129 us (21%)
  starting transfers between devices  43.5 us (7%)
  matrix products  7.07 us (1%)
    ppermute x12, waiting for transfers between devices, gather_edges(): lax.ppermute(edge_set, 'ty', [(dev, dev ^ hop) for dev in range(16)])  292 us
    add x2, other arithmetic, laplace(): metric[0] * (padded_x[..., :-2] - source)  68.3 us
    add x1, other arithmetic, per_device(): fields - damp_four[:, None, None, None] * fourth  35.4 us
    unnamed x28, local copies, waits for them, and re-layouts  28.6 us
    ppermute x12, starting transfers between devices, gather_edges(): lax.ppermute(edge_set, 'ty', [(dev, dev ^ hop) for dev in range(16)])  23.4 us
    slice x4, local copies, waits for them, and re-layouts, strip_edges(): east_cells = jnp.transpose(source[:, :, :, -1], (0, 2, 1))  18.6 us
    add x1, local copies, waits for them, and re-layouts, per_device(): fields - damp_four[:, None, None, None] * fourth  18.5 us
    broadcast_in_dim x6, local copies, waits for them, and re-layouts, laplace(): jnp.transpose(lax.dynamic_slice_in_dim(halo_cells[:, :, 1], row_start, st...  15.9 us
  transfers between devices with their start and end apart: 18, of which 12 were waited for; matrix products, arithmetic and copies ran while one was open for 13% of the time, Pallas kernels for 0%

profile of v1, /device:TPU:0, one launch (start us, length us, event | category | flops | bytes accessed | tf_op | source)
XLA Modules:
  0.0 617.7 jit_solution(9163846853558585950)
XLA Ops:
  0.0 4.6 fusion.60
  4.6 18.5 %copy.87 = f32[16,48,6,768]{3,0,2,1:T(8,128)} copy(f32[16,48,6,768]{3,1,2,0:T(8,128)} %param.5) | data formatting | bytes 28311552 | tf_op args[0]
  36.7 26.3 %collective-permute-done.1 = f32[16,6,4,768]{3,0,2,1:T(8,128)S(1)} collective-permute-done((f32[16,6,4,768]{3,0,2,1:T(8,128)S(1)}, f32[16,6,4,768]{3,0,2,1:T(8,128)S(1)}, u32[]{:S(2)}, u32[]{:S(2)}) %collective-permute-start.1) | collective-permute-done | bytes 1179680 | tf_op jit(solution)/shard_map/ppermute | solution.py:43
  65.2 25.6 %collective-permute-done.2 = f32[16,6,4,768]{3,0,2,1:T(8,128)S(1)} collective-permute-done((f32[16,6,4,768]{3,0,2,1:T(8,128)S(1)}, f32[16,6,4,768]{3,0,2,1:T(8,128)S(1)}, u32[]{:S(2)}, u32[]{:S(2)}) %collective-permute-start.2) | collective-permute-done | bytes 1179680 | tf_op jit(solution)/shard_map/ppermute | solution.py:43
  101.7 43.3 %collective-permute-done.3 = f32[16,6,4,768]{3,0,2,1:T(8,128)} collective-permute-done((f32[16,6,4,768]{3,0,2,1:T(8,128)}, f32[16,6,4,768]{3,0,2,1:T(8,128)}, u32[]{:S(2)}, u32[]{:S(2)}) %collective-permute-start.3) | collective-permute-done | bytes 1179680 | tf_op jit(solution)/shard_map/ppermute | solution.py:43
  154.4 4.7 rev.9
  169.2 4.0 copy.70
  175.2 33.6 %fusion.26 = f32[16,48,6,768]{3,0,2,1:T(8,128)} fusion(f32[16,48,6,768]{3,0,2,1:T(8,128)} %copy.87, f32[16,1,6,768]{3,0,2,1:T(8,128)} %get-tuple-element.38, f32[16,1,6,768]{3,0,2,1:T(8,128)} %get-tuple-element.37, f32[16,48,6,1]{3,0,2,1:T(8,128)} %copy.70, f32[16,48,6,1]{3,0,2,1:T(8,128)} %copy.65, f32[48,6,768]{2,1,0:T(8,128)} %copy.75, ...), kind=kLoop, calls=%fused_computation.35 | loop fusion | flops 53084160 | bytes 32477184 | tf_op jit(solution)/shard_map/add | solution.py:77
  208.8 5.3 fusion.58
  234.4 26.3 %collective-permute-done.7 = f32[16,6,4,768]{3,0,1,2:T(8,128)S(1)} collective-permute-done((f32[16,6,4,768]{3,0,1,2:T(8,128)S(1)}, f32[16,6,4,768]{3,0,1,2:T(8,128)S(1)}, u32[]{:S(2)}, u32[]{:S(2)}) %collective-permute-start.7) | collective-permute-done | bytes 1179680 | tf_op jit(solution)/shard_map/ppermute | solution.py:43
  262.1 26.4 %collective-permute-done.8 = f32[16,6,4,768]{3,0,1,2:T(8,128)S(1)} collective-permute-done((f32[16,6,4,768]{3,0,1,2:T(8,128)S(1)}, f32[16,6,4,768]{3,0,1,2:T(8,128)S(1)}, u32[]{:S(2)}, u32[]{:S(2)}) %collective-permute-start.8) | collective-permute-done | bytes 1179680 | tf_op jit(solution)/shard_map/ppermute | solution.py:43
  293.1 11.0 %collective-permute-start.11 = (f32[16,1,6,768]{3,0,2,1:T(8,128)}, f32[16,1,6,768]{3,0,2,1:T(8,128)}, u32[]{:S(2)}, u32[]{:S(2)}) collective-permute-start(f32[16,1,6,768]{3,0,2,1:T(8,128)} %get-tuple-element.14), channel_id=1, source_target_pairs={{1,0},{2,1},{3,2},{4,3},{5,4},{6,5},{7,6},{8,7},{9,8},{10,9},{11,1... | collective-permute-start | bytes 884744 | tf_op jit(solution)/shard_map/ppermute | solution.py:17
  304.1 37.3 %collective-permute-done.9 = f32[16,6,4,768]{3,0,1,2:T(8,128)S(1)} collective-permute-done((f32[16,6,4,768]{3,0,1,2:T(8,128)S(1)}, f32[16,6,4,768]{3,0,1,2:T(8,128)S(1)}, u32[]{:S(2)}, u32[]{:S(2)}) %collective-permute-start.9) | collective-permute-done | bytes 1179680 | tf_op jit(solution)/shard_map/ppermute | solution.py:43
  349.3 4.8 rev.10
  364.1 4.0 copy.86
  370.1 34.7 %fusion.15 = f32[16,48,6,768]{3,0,2,1:T(8,128)} fusion(f32[16,48,6,768]{3,0,2,1:T(8,128)} %fusion.26, f32[16,1,6,768]{3,0,2,1:T(8,128)} %get-tuple-element.34, f32[16,1,6,768]{3,0,2,1:T(8,128)} %get-tuple-element.33, f32[16,48,6,1]{3,0,2,1:T(8,128)} %copy.86, f32[16,48,6,1]{3,0,2,1:T(8,128)} %copy.85, f32[48,6,768]{2,1,0:T(8,128)} %copy.75, ...), kind=kLoop, calls=%fused_computation.20 | loop fusion | flops 53084160 | bytes 32477184 | tf_op jit(solution)/shard_map/add | solution.py:77
  404.7 5.3 fusion.56
  430.5 26.3 %collective-permute-done.13 = f32[16,6,4,768]{3,0,2,1:T(8,128)S(1)} collective-permute-done((f32[16,6,4,768]{3,0,2,1:T(8,128)S(1)}, f32[16,6,4,768]{3,0,2,1:T(8,128)S(1)}, u32[]{:S(2)}, u32[]{:S(2)}) %collective-permute-start.13) | collective-permute-done | bytes 1179680 | tf_op jit(solution)/shard_map/ppermute | solution.py:43
  458.1 26.4 %collective-permute-done.14 = f32[16,6,4,768]{3,0,2,1:T(8,128)S(1)} collective-permute-done((f32[16,6,4,768]{3,0,2,1:T(8,128)S(1)}, f32[16,6,4,768]{3,0,2,1:T(8,128)S(1)}, u32[]{:S(2)}, u32[]{:S(2)}) %collective-permute-start.14) | collective-permute-done | bytes 1179680 | tf_op jit(solution)/shard_map/ppermute | solution.py:43
  490.6 46.9 %collective-permute-done.15 = f32[16,6,4,768]{3,0,2,1:T(8,128)S(1)} collective-permute-done((f32[16,6,4,768]{3,0,2,1:T(8,128)S(1)}, f32[16,6,4,768]{3,0,2,1:T(8,128)S(1)}, u32[]{:S(2)}, u32[]{:S(2)}) %collective-permute-start.15) | collective-permute-done | bytes 1179680 | tf_op jit(solution)/shard_map/ppermute | solution.py:43
  545.3 4.7 rev.11
  557.8 4.0 copy.95
  563.3 35.4 %fusion.4 = f32[16,48,6,768]{3,0,2,1:T(8,128)} fusion(f32[16,48,6,768]{3,0,2,1:T(8,128)} %fusion.15, f32[16,1,6,768]{3,0,2,1:T(8,128)S(1)} %get-tuple-element.30, f32[16,1,6,768]{3,0,2,1:T(8,128)S(1)} %get-tuple-element.29, f32[16,48,6,1]{3,0,2,1:T(8,128)} %copy.95, f32[16,48,6,1]{3,0,2,1:T(8,128)} %copy.94, f32[16]{0:T(128)S(1)} %copy-done.10, ...), kind=kLoop, calls=%fused_computation.5 | loop fusion | flops 67239936 | bytes 46633088 | tf_op jit(solution)/shard_map/add | solution.py:88
  598.7 18.5 %copy.96 = f32[16,48,6,768]{3,1,2,0:T(8,128)} copy(f32[16,48,6,768]{3,0,2,1:T(8,128)} %fusion.4) | data formatting | bytes 28311552 | tf_op jit(solution)/shard_map/add | solution.py:88
  (122 shorter events, 139.0 us)
Async XLA Ops:
  29.0 4.6 collective-permute-start
  33.8 29.2 %collective-permute-start.1 = (f32[16,6,4,768]{3,0,2,1:T(8,128)S(1)}, f32[16,6,4,768]{3,0,2,1:T(8,128)S(1)}, u32[]{:S(2)}, u32[]{:S(2)}) collective-permute-start(f32[16,6,4,768]{3,0,2,1:T(8,128)S(1)} %fusion.54), channel_id=1, source_target_pairs={{0,2},{1,3},{2,0},{3,1},{4,6},{5,7},{6,4},{7,5},{8,10},{9,11},{10,... | collective-permute-start | bytes 3538952 | tf_op jit(solution)/shard_map/ppermute | solution.py:43
  63.0 35.1 %copy-start.9 = (s32[6,4,3]{0,1,2:T(4,128)S(1)}, s32[6,4,3]{0,1,2:T(4,128)}, u32[]{:S(2)}) copy-start(s32[6,4,3]{0,1,2:T(4,128)} %param.9) | copy-start | bytes 868
  63.3 35.0 %copy-start.8 = (f32[4,48,6,768]{3,1,2,0:T(8,128)S(1)}, f32[4,48,6,768]{3,1,2,0:T(8,128)}, u32[]{:S(2)}) copy-start(f32[4,48,6,768]{3,1,2,0:T(8,128)} %param.8) | copy-start | bytes 10616836
  63.3 27.5 %collective-permute-start.2 = (f32[16,6,4,768]{3,0,2,1:T(8,128)S(1)}, f32[16,6,4,768]{3,0,2,1:T(8,128)S(1)}, u32[]{:S(2)}, u32[]{:S(2)}) collective-permute-start(f32[16,6,4,768]{3,0,2,1:T(8,128)S(1)} %fusion.69), channel_id=1, source_target_pairs={{0,4},{1,5},{2,6},{3,7},{4,0},{5,1},{6,2},{7,3},{8,12},{9,13},{10,... | collective-permute-start | bytes 3538952 | tf_op jit(solution)/shard_map/ppermute | solution.py:43
  92.0 53.1 %collective-permute-start.3 = (f32[16,6,4,768]{3,0,2,1:T(8,128)}, f32[16,6,4,768]{3,0,2,1:T(8,128)}, u32[]{:S(2)}, u32[]{:S(2)}) collective-permute-start(f32[16,6,4,768]{3,0,2,1:T(8,128)} %add.92), channel_id=1, source_target_pairs={{0,8},{1,9},{2,10},{3,11},{4,12},{5,13},{6,14},{7,15},{8,0},{9,1},... | collective-permute-start | bytes 3538952 | tf_op jit(solution)/shard_map/ppermute | solution.py:43
  94.6 78.6 %collective-permute-start.4 = (f32[16,1,6,768]{3,0,2,1:T(8,128)}, f32[16,1,6,768]{3,0,2,1:T(8,128)}, u32[]{:S(2)}, u32[]{:S(2)}) collective-permute-start(f32[16,1,6,768]{3,0,2,1:T(8,128)} %get-tuple-element.17), channel_id=1, source_target_pairs={{0,1},{1,2},{2,3},{3,4},{4,5},{5,6},{6,7},{7,8},{8,9},{9,10},{10,1... | collective-permute-start | bytes 884744 | tf_op jit(solution)/shard_map/ppermute | solution.py:15
  96.6 76.6 %collective-permute-start.5 = (f32[16,1,6,768]{3,0,2,1:T(8,128)}, f32[16,1,6,768]{3,0,2,1:T(8,128)}, u32[]{:S(2)}, u32[]{:S(2)}) collective-permute-start(f32[16,1,6,768]{3,0,2,1:T(8,128)} %get-tuple-element.19), channel_id=1, source_target_pairs={{1,0},{2,1},{3,2},{4,3},{5,4},{6,5},{7,6},{8,7},{9,8},{10,9},{11,1... | collective-permute-start | bytes 884744 | tf_op jit(solution)/shard_map/ppermute | solution.py:17
  228.4 3.6 collective-permute-start.6
  232.2 28.5 %collective-permute-start.7 = (f32[16,6,4,768]{3,0,1,2:T(8,128)S(1)}, f32[16,6,4,768]{3,0,1,2:T(8,128)S(1)}, u32[]{:S(2)}, u32[]{:S(2)}) collective-permute-start(f32[16,6,4,768]{3,0,1,2:T(8,128)S(1)} %fusion.53), channel_id=1, source_target_pairs={{0,2},{1,3},{2,0},{3,1},{4,6},{5,7},{6,4},{7,5},{8,10},{9,11},{10,... | collective-permute-start | bytes 3538952 | tf_op jit(solution)/shard_map/ppermute | solution.py:43
  261.0 27.5 %collective-permute-start.8 = (f32[16,6,4,768]{3,0,1,2:T(8,128)S(1)}, f32[16,6,4,768]{3,0,1,2:T(8,128)S(1)}, u32[]{:S(2)}, u32[]{:S(2)}) collective-permute-start(f32[16,6,4,768]{3,0,1,2:T(8,128)S(1)} %fusion.68), channel_id=1, source_target_pairs={{0,4},{1,5},{2,6},{3,7},{4,0},{5,1},{6,2},{7,3},{8,12},{9,13},{10,... | collective-permute-start | bytes 3538952 | tf_op jit(solution)/shard_map/ppermute | solution.py:43
  288.6 52.8 %collective-permute-start.9 = (f32[16,6,4,768]{3,0,1,2:T(8,128)S(1)}, f32[16,6,4,768]{3,0,1,2:T(8,128)S(1)}, u32[]{:S(2)}, u32[]{:S(2)}) collective-permute-start(f32[16,6,4,768]{3,0,1,2:T(8,128)S(1)} %add.101), channel_id=1, source_target_pairs={{0,8},{1,9},{2,10},{3,11},{4,12},{5,13},{6,14},{7,15},{8,0},{9,1},... | collective-permute-start | bytes 3538952 | tf_op jit(solution)/shard_map/ppermute | solution.py:43
  291.1 77.0 %collective-permute-start.10 = (f32[16,1,6,768]{3,0,2,1:T(8,128)}, f32[16,1,6,768]{3,0,2,1:T(8,128)}, u32[]{:S(2)}, u32[]{:S(2)}) collective-permute-start(f32[16,1,6,768]{3,0,2,1:T(8,128)} %get-tuple-element.11), channel_id=1, source_target_pairs={{0,1},{1,2},{2,3},{3,4},{4,5},{5,6},{6,7},{7,8},{8,9},{9,10},{10,1... | collective-permute-start | bytes 884744 | tf_op jit(solution)/shard_map/ppermute | solution.py:15
  293.1 75.0 %collective-permute-start.11 = (f32[16,1,6,768]{3,0,2,1:T(8,128)}, f32[16,1,6,768]{3,0,2,1:T(8,128)}, u32[]{:S(2)}, u32[]{:S(2)}) collective-permute-start(f32[16,1,6,768]{3,0,2,1:T(8,128)} %get-tuple-element.14), channel_id=1, source_target_pairs={{1,0},{2,1},{3,2},{4,3},{5,4},{6,5},{7,6},{8,7},{9,8},{10,9},{11,1... | collective-permute-start | bytes 884744 | tf_op jit(solution)/shard_map/ppermute | solution.py:17
  423.1 1.2 copy-start.2
  424.4 3.7 collective-permute-start.12
  428.3 28.5 %collective-permute-start.13 = (f32[16,6,4,768]{3,0,2,1:T(8,128)S(1)}, f32[16,6,4,768]{3,0,2,1:T(8,128)S(1)}, u32[]{:S(2)}, u32[]{:S(2)}) collective-permute-start(f32[16,6,4,768]{3,0,2,1:T(8,128)S(1)} %fusion.52), channel_id=1, source_target_pairs={{0,2},{1,3},{2,0},{3,1},{4,6},{5,7},{6,4},{7,5},{8,10},{9,11},{10,... | collective-permute-start | bytes 3538952 | tf_op jit(solution)/shard_map/ppermute | solution.py:43
  457.0 27.5 %collective-permute-start.14 = (f32[16,6,4,768]{3,0,2,1:T(8,128)S(1)}, f32[16,6,4,768]{3,0,2,1:T(8,128)S(1)}, u32[]{:S(2)}, u32[]{:S(2)}) collective-permute-start(f32[16,6,4,768]{3,0,2,1:T(8,128)S(1)} %fusion.67), channel_id=1, source_target_pairs={{0,4},{1,5},{2,6},{3,7},{4,0},{5,1},{6,2},{7,3},{8,12},{9,13},{10,... | collective-permute-start | bytes 3538952 | tf_op jit(solution)/shard_map/ppermute | solution.py:43
  484.7 52.8 %collective-permute-start.15 = (f32[16,6,4,768]{3,0,2,1:T(8,128)S(1)}, f32[16,6,4,768]{3,0,2,1:T(8,128)S(1)}, u32[]{:S(2)}, u32[]{:S(2)}) collective-permute-start(f32[16,6,4,768]{3,0,2,1:T(8,128)S(1)} %add.108), channel_id=1, source_target_pairs={{0,8},{1,9},{2,10},{3,11},{4,12},{5,13},{6,14},{7,15},{8,0},{9,1},... | collective-permute-start | bytes 3538952 | tf_op jit(solution)/shard_map/ppermute | solution.py:43
  487.1 74.6 %collective-permute-start.16 = (f32[16,1,6,768]{3,0,2,1:T(8,128)}, f32[16,1,6,768]{3,0,2,1:T(8,128)}, u32[]{:S(2)}, u32[]{:S(2)}) collective-permute-start(f32[16,1,6,768]{3,0,2,1:T(8,128)} %get-tuple-element.5), channel_id=1, source_target_pairs={{0,1},{1,2},{2,3},{3,4},{4,5},{5,6},{6,7},{7,8},{8,9},{9,10},{10,1... | collective-permute-start | bytes 884744 | tf_op jit(solution)/shard_map/ppermute | solution.py:15
  489.1 72.7 %collective-permute-start.17 = (f32[16,1,6,768]{3,0,2,1:T(8,128)}, f32[16,1,6,768]{3,0,2,1:T(8,128)}, u32[]{:S(2)}, u32[]{:S(2)}) collective-permute-start(f32[16,1,6,768]{3,0,2,1:T(8,128)} %get-tuple-element.8), channel_id=1, source_target_pairs={{1,0},{2,1},{3,2},{4,3},{5,4},{6,5},{7,6},{8,7},{9,8},{10,9},{11,1... | collective-permute-start | bytes 884744 | tf_op jit(solution)/shard_map/ppermute | solution.py:17
  561.7 1.5 copy-start
  561.7 1.5 copy-start.10
  561.8 1.5 copy-start.11
  (6 other events, 6.6 us)
